TPU v7x, 32 devices: a whole 2x2x4 slice. The times are simulated.
32 devices in a mesh: replica: 8 (over y, x, core), tensor: 4 (over z).
Axes of the slice: x: 2, y: 2, z: 4, core: 2. Of those that a mesh axis runs over, the one named last changes fastest.
Arguments:
- queries: bfloat16 [8, 512, 2560], P('replica', None, 'tensor'), may hold values from -160 to 160
- key_rows: bfloat16 [8, 512, 2560], P('replica', None, 'tensor'), may hold values from -4 to 4
- value_rows: bfloat16 [8, 512, 2560], P('replica', None, 'tensor'), may hold values from -6 to 6
- out_grads: bfloat16 [8, 512, 1024], P('replica', 'tensor'), may hold values from -6 to 6
- inner_weights: bfloat16 [8, 20, 128, 1024], P('replica', 'tensor'), may hold values from -0.15625 to 0.15625
- adam_first: bfloat16 [8, 20, 128, 1024], P('replica', 'tensor'), may hold values from -12 to 12
- adam_second: bfloat16 [8, 20, 128, 1024], P('replica', 'tensor'), may hold values from 1 to 16
- anchor: bfloat16 [20, 128, 1024], P('tensor'), may hold values from -0.125 to 0.125
- momentum: float32 [20, 128, 1024], P('tensor', 'replica'), may hold values from -0.06 to 0.06
Outputs:
- query_grads: bfloat16 [8, 512, 2560], P('replica', None, 'tensor')
- key_grads: bfloat16 [8, 512, 2560], P('replica', None, 'tensor')
- value_grads: bfloat16 [8, 512, 2560], P('replica', None, 'tensor')
- new_first: bfloat16 [8, 20, 128, 1024], P('replica', 'tensor')
- new_second: bfloat16 [8, 20, 128, 1024], P('replica', 'tensor')
- new_anchor: bfloat16 [20, 128, 1024], P('tensor')
- new_momentum: float32 [20, 128, 1024], P('tensor', 'replica')
All inputs are finite; a program needn't handle non-finite values.
Results may differ from a plain program's by a relative error of at most 0.028.
Values may be sent and summed in bfloat16 or wider, within the bound.
A program may use at most 64 MiB of HBM per device.

v0:
```python
import functools
import math

import jax
import jax.numpy as jnp
from jax import lax
from jax.experimental import pallas as pl
from jax.experimental.pallas import tpu as pltpu
from jax.sharding import PartitionSpec as P

DH = 128
CHUNKS = 2
TILE = 512
VMEM_BYTES = 67043328
SPARE = 2**17
MESH = pl.DeviceIdType.MESH

beta_first = 0.9
beta_second = 0.95
correct_first = 0.9999734386011124
correct_second = 0.994079470779666
inner_rate = 0.01
decay_rate = 0.1
epsilon = 1e-08
outer_rate = 0.7
outer_beta = 0.9

F32 = jnp.float32
BF16 = jnp.bfloat16


def dot(a, b, ca, cb):
    return lax.dot_general(a, b, (((ca,), (cb,)), ((), ())), preferred_element_type=F32)


def kernel(
    tensors,
    workers,
    q_hbm, k_hbm, v_hbm, g_hbm, w_hbm, m1_hbm, m2_hbm, anchor_hbm, mom_hbm,
    dq, dk, dv, n1, n2, na, nm,
    q, k, v, g, w, m1, m2, anchor, mom,
    probs, att, att_t, ds, delta, from_partner, pair, from_peers,
    in_sem,
    g_send, g_recv, p_send, p_recv, r_send, r_recv, a_send, a_recv, f_send, f_recv,
):
    heads = w.shape[0]
    width = g.shape[2]
    length = q.shape[0]
    rows = g.shape[1]
    slab = mom.shape[1]
    chips = workers // 2
    cw = width // CHUNKS
    scale = 1.0 / math.sqrt(DH)

    i = lax.axis_index("tensor")
    r = lax.axis_index("replica")
    chip = r // 2
    core = r % 2
    partner = chip * 2 + 1 - core
    has_left = i > 0
    has_right = i < tensors - 1

    def peer(step):
        return lax.rem(chip + step, chips) * 2 + core

    def source(step):
        return lax.rem(chip + chips - step, chips)

    barrier = pltpu.get_barrier_semaphore()

    @pl.when(has_left)
    def _():
        pl.semaphore_signal(barrier, inc=1, device_id={"tensor": i - 1}, device_id_type=MESH)

    @pl.when(has_right)
    def _():
        pl.semaphore_signal(barrier, inc=1, device_id={"tensor": i + 1}, device_id_type=MESH)

    pl.semaphore_signal(barrier, inc=1, device_id={"replica": partner}, device_id_type=MESH)
    for step in range(1, chips):
        pl.semaphore_signal(barrier, inc=1, device_id={"replica": peer(step)}, device_id_type=MESH)

    loads = [
        pltpu.make_async_copy(s, d, in_sem.at[n])
        for n, (s, d) in enumerate(
            [
                (q_hbm, q), (k_hbm, k), (v_hbm, v), (g_hbm, g.at[i]), (w_hbm, w),
                (m1_hbm, m1), (m2_hbm, m2), (anchor_hbm, anchor), (mom_hbm, mom),
            ]
        )
    ]
    for load in loads:
        load.start()

    inner = jnp.logical_and(has_left, has_right)

    @pl.when(inner)
    def _():
        pl.semaphore_wait(barrier, chips + 2)

    @pl.when(jnp.logical_not(inner))
    def _():
        pl.semaphore_wait(barrier, chips + 1)

    def cols(c):
        return pl.ds(c * cw, cw)

    def right_copy(block, s, c, own=False):
        src = g_hbm.at[:, cols(c)] if own else g.at[block, :, cols(c)]
        return pltpu.make_async_remote_copy(
            src_ref=src, dst_ref=g.at[block, :, cols(c)],
            send_sem=g_send.at[0, s, c], recv_sem=g_recv.at[0, s, c],
            device_id={"tensor": i + 1}, device_id_type=MESH,
        )

    def left_copy(block, s, c, own=False):
        src = g_hbm.at[:, cols(c)] if own else g.at[block, :, cols(c)]
        return pltpu.make_async_remote_copy(
            src_ref=src, dst_ref=g.at[block, :, cols(c)],
            send_sem=g_send.at[1, s, c], recv_sem=g_recv.at[1, s, c],
            device_id={"tensor": i - 1}, device_id_type=MESH,
        )

    def own_send(c):
        @pl.when(has_right)
        def _():
            right_copy(i, 0, c, True).start()

        @pl.when(has_left)
        def _():
            left_copy(i, 0, c, True).start()

    def relay(c, s):
        @pl.when(i - 1 - s >= 0)
        def _():
            block = i - 1 - s
            right_copy(block, s, c).wait_recv()
            if s + 1 <= tensors - 2:
                @pl.when(has_right)
                def _():
                    right_copy(block, s + 1, c).start()

        @pl.when(i + 1 + s < tensors)
        def _():
            block = i + 1 + s
            left_copy(block, s, c).wait_recv()
            if s + 1 <= tensors - 2:
                @pl.when(has_left)
                def _():
                    left_copy(block, s + 1, c).start()

    def drain_gather():
        for c in range(CHUNKS):
            for s in range(tensors - 1):
                @pl.when(jnp.logical_and(has_right, i - s >= 0))
                def _():
                    right_copy(i - s, s, c, s == 0).wait_send()

                @pl.when(jnp.logical_and(has_left, i + s < tensors))
                def _():
                    left_copy(i + s, s, c, s == 0).wait_send()

    tile = TILE

    def forward(h):
        hc = pl.ds(h * DH, DH)
        kh = k[:, hc]
        vh = v[:, hc]
        for t in range(length // tile):
            tr = pl.ds(t * tile, tile)
            s = dot(q[tr, hc], kh, 1, 1) * scale
            e = jnp.exp(s - jnp.max(s, axis=-1, keepdims=True))
            p = (e / jnp.sum(e, axis=-1, keepdims=True)).astype(BF16)
            probs[h, tr, :] = p
            a = dot(p, vh, 1, 0)
            att[tr, hc] = a.astype(BF16)
            att_t[h, :, tr] = a.T.astype(BF16)

    def adam(c):
        def body(h, carry):
            gb = g[:, :, cols(c)].reshape(length, cw)
            grad = dot(att_t[h], gb, 1, 0)
            first = beta_first * m1[h, :, cols(c)].astype(F32) + (1.0 - beta_first) * grad
            second = (
                beta_second * m2[h, :, cols(c)].astype(F32) + (1.0 - beta_second) * grad * grad
            )
            n1[h, :, cols(c)] = first.astype(BF16)
            n2[h, :, cols(c)] = second.astype(BF16)
            old = w[h, :, cols(c)].astype(F32)
            stepped = old - inner_rate * (
                first / correct_first / (jnp.sqrt(second / correct_second) + epsilon)
                + decay_rate * old
            )
            an = anchor[h, :, :, cols(c)].astype(F32)
            d = an - stepped.reshape(workers, slab, cw)
            for x in range(workers):
                delta[c, x % 2, x // 2, h] = d[x].astype(BF16)
            return carry

        lax.fori_loop(0, heads, body, 0)

    def partner_copy(c):
        return pltpu.make_async_remote_copy(
            src_ref=delta.at[c, 1 - core], dst_ref=from_partner.at[c],
            send_sem=p_send.at[c], recv_sem=p_recv.at[c],
            device_id={"replica": partner}, device_id_type=MESH,
        )

    def peer_copy(c, step):
        return pltpu.make_async_remote_copy(
            src_ref=pair.at[c, lax.rem(chip + step, chips)], dst_ref=from_peers.at[c, step - 1],
            send_sem=r_send.at[c, step - 1], recv_sem=r_recv.at[c, step - 1],
            device_id={"replica": peer(step)}, device_id_type=MESH,
        )

    def pair_sum(c):
        partner_copy(c).wait_recv()
        for x in range(chips):
            pair[c, x] = (
                delta[c, core, x].astype(F32) + from_partner[c, x].astype(F32)
            ).astype(BF16)
        for step in range(1, chips):
            peer_copy(c, step).start()

    def spread(c, block, step):
        return pltpu.make_async_remote_copy(
            src_ref=na.at[:, block, :, cols(c)], dst_ref=na.at[:, block, :, cols(c)],
            send_sem=a_send.at[c, step - 1], recv_sem=a_recv.at[c, step - 1],
            device_id={"replica": peer(step)}, device_id_type=MESH,
        )

    def across(c, block, step):
        return pltpu.make_async_remote_copy(
            src_ref=na.at[:, block, :, cols(c)], dst_ref=na.at[:, block, :, cols(c)],
            send_sem=f_send.at[c, step], recv_sem=f_recv.at[c, step],
            device_id={"replica": partner}, device_id_type=MESH,
        )

    def outer(c):
        total = delta[c, core, chip].astype(F32) + from_partner[c, chip].astype(F32)
        for step in range(1, chips):
            peer_copy(c, step).wait_recv()
            total = total + from_peers[c, step - 1].astype(F32)
        average = total / workers
        moved = outer_beta * mom[:, :, cols(c)] + average
        nm[:, :, cols(c)] = moved
        part = anchor[:, r, :, cols(c)].astype(F32)
        na[:, r, :, cols(c)] = (
            part - outer_rate * (average + outer_beta * moved)
        ).astype(BF16)
        for step in range(1, chips):
            spread(c, r, step).start()
        across(c, r, 0).start()

    def pass_on(c):
        for step in range(1, chips):
            block = source(step) * 2 + core
            spread(c, block, step).wait_recv()
            across(c, block, step).start()

    def finish(c):
        for step in range(chips):
            across(c, source(step) * 2 + 1 - core, step).wait_recv()

    def backward(h):
        hc = pl.ds(h * DH, DH)
        kh = k[:, hc]
        vh = v[:, hc]
        ga = dot(g[...].reshape(length, width), w[h], 1, 1).astype(BF16)
        for t in range(length // tile):
            tr = pl.ds(t * tile, tile)
            gt = ga[t * tile:(t + 1) * tile]
            row = jnp.sum(gt.astype(F32) * att[tr, hc].astype(F32), axis=-1, keepdims=True)
            gp = dot(gt, vh, 1, 1)
            s = (probs[h, tr, :].astype(F32) * (gp - row)).astype(BF16)
            ds[tr, :] = s
            dq[tr, hc] = (dot(s, kh, 1, 0) * scale).astype(BF16)
        dv[:, hc] = dot(ga, probs[h], 0, 0).T.astype(BF16)
        dk[:, hc] = (dot(q[:, hc], ds[...], 0, 0) * scale).T.astype(BF16)

    ahead = min(2, CHUNKS)
    for c in range(ahead):
        own_send(c)
    for load in loads[:3]:
        load.wait()
    for h in range(heads):
        forward(h)
        if h < tensors - 1:
            relay(0, h)
    for s in range(heads, tensors - 1):
        relay(0, s)
    for load in loads[3:]:
        load.wait()
    for c in range(CHUNKS):
        if c > 0:
            for s in range(tensors - 1):
                if s == tensors - 2:
                    pair_sum(c - 1)
                relay(c, s)
        if c + ahead < CHUNKS:
            own_send(c + ahead)
        adam(c)
        partner_copy(c).start()
        if c > 0:
            outer(c - 1)
        if 0 < c < CHUNKS - 1:
            pass_on(c - 1)
    last = CHUNKS - 1
    for h in range(heads):
        backward(h)
        if h == 0:
            pair_sum(last)
        if h == min(1, heads - 1):
            if CHUNKS > 1:
                pass_on(last - 1)
            outer(last)
        if h == min(3, heads - 1):
            pass_on(last)
    for c in range(CHUNKS):
        finish(c)
    drain_gather()
    for c in range(CHUNKS):
        partner_copy(c).wait_send()
        for step in range(1, chips):
            peer_copy(c, step).wait_send()
            spread(c, r, step).wait_send()
        for step in range(chips):
            across(c, source(step) * 2 + core, step).wait_send()

def store(*refs):
    n = (len(refs) - 1) // 2
    copies = [pltpu.make_async_copy(refs[j], refs[n + j], refs[-1].at[j]) for j in range(n)]
    for copy in copies:
        copy.start()
    for copy in copies:
        copy.wait()


def local(tensors, workers, queries, key_rows, value_rows, out_grads, inner_weights, adam_first,
          adam_second, anchor, momentum):
    length, inner = queries.shape[1:]
    rows, width = out_grads.shape[1:]
    heads = inner_weights.shape[1]
    slab = momentum.shape[1]
    chips = workers // 2
    cw = width // CHUNKS
    qs = (length, inner)
    ws = (heads, DH, width)
    an = (heads, workers, slab, width)
    ms = (heads, slab, width)
    S = jax.ShapeDtypeStruct
    hbm = pl.BlockSpec(memory_space=pltpu.HBM)
    V = pltpu.VMEM
    D = pltpu.SemaphoreType.DMA
    results = [(qs, BF16)] * 3 + [(ws, BF16)] * 2 + [(an, BF16), (ms, F32)]
    held = sum(math.prod(shape) * jnp.dtype(dtype).itemsize for shape, dtype in results)
    room = VMEM_BYTES - held - SPARE
    outs = pl.pallas_call(
        functools.partial(kernel, tensors, workers),
        out_shape=[V(shape, dtype) for shape, dtype in results],
        in_specs=[hbm] * 9,
        out_specs=[pl.BlockSpec(memory_space=V)] * 7,
        scratch_shapes=[
            V(qs, BF16), V(qs, BF16), V(qs, BF16), V((tensors, rows, width), BF16),
            V(ws, BF16), V(ws, BF16), V(ws, BF16), V(an, BF16), V(ms, F32),
            V((heads, length, length), BF16), V(qs, BF16), V((heads, DH, length), BF16),
            V((length, length), BF16),
            V((CHUNKS, 2, chips, heads, slab, cw), BF16),
            V((CHUNKS, chips, heads, slab, cw), BF16),
            V((CHUNKS, chips, heads, slab, cw), BF16),
            V((CHUNKS, chips - 1, heads, slab, cw), BF16),
            D((9,)),
            D((2, tensors - 1, CHUNKS)), D((2, tensors - 1, CHUNKS)),
            D((CHUNKS,)), D((CHUNKS,)),
            D((CHUNKS, chips - 1)), D((CHUNKS, chips - 1)),
            D((CHUNKS, chips - 1)), D((CHUNKS, chips - 1)),
            D((CHUNKS, chips)), D((CHUNKS, chips)),
        ],
        compiler_params=pltpu.CompilerParams(collective_id=0, has_side_effects=True, vmem_limit_bytes=room),
        name="sync",
    )(
        queries[0], key_rows[0], value_rows[0], out_grads[0], inner_weights[0], adam_first[0],
        adam_second[0], anchor.reshape(an), momentum,
    )
    dq, dk, dv, n1, n2, na, nm = pl.pallas_call(
        store,
        out_shape=[S(shape, dtype) for shape, dtype in results],
        in_specs=[pl.BlockSpec(memory_space=V)] * 7,
        out_specs=[hbm] * 7,
        scratch_shapes=[D((7,))],
        compiler_params=pltpu.CompilerParams(vmem_limit_bytes=2**20),
        name="store",
    )(*outs)
    return dq[None], dk[None], dv[None], n1[None], n2[None], na.reshape(anchor.shape), nm


def solution(mesh):
    workers = P("replica", "tensor", None, None)
    heads = P("replica", None, "tensor")
    specs = (
        heads, heads, heads, P("replica", "tensor", None), workers, workers, workers,
        P("tensor", None, None), P("tensor", "replica", None),
    )
    outs = (
        heads, heads, heads, workers, workers, P("tensor", None, None), P("tensor", "replica", None)
    )
    body = functools.partial(local, mesh.shape["tensor"], mesh.shape["replica"])
    return jax.shard_map(body, mesh=mesh, in_specs=specs, out_specs=outs, check_vma=False)
```

profile of v0, /device:TPU:0, one launch (start us, length us, event | category | flops | bytes accessed | tf_op | source)
XLA Modules:
  0.0 49.7 jit_solution(12479068054830374497)
XLA Ops:
  0.6 46.3 %sync.1 = (bf16[512,640]{1,0:T(8,128)(2,1)S(1)}, bf16[512,640]{1,0:T(8,128)(2,1)S(1)}, bf16[512,640]{1,0:T(8,128)(2,1)S(1)}, bf16[5,128,1024]{2,1,0:T(8,128)(2,1...) custom-call(bf16[512,640]{1,0:T(8,128)(2,1)} %bitcast.18, ...), custom_call_target="tpu_custom_call" | custom-call | tf_op jit(solution)/shard_map/sync/pallas_call | solution.py:358
  47.0 2.7 %store.1 = (bf16[512,640]{1,0:T(8,128)(2,1)}, bf16[512,640]{1,0:T(8,128)(2,1)}, bf16[512,640]{1,0:T(8,128)(2,1)}, bf16[5,128,1024]{2,1,0:T(8,128)(2,1)}, bf16[5,...) custom-call(bf16[512,640]{1,0:T(8,128)(2,1)S(1)} %get-tuple-element.21.refs_0_, ...), custom_call_target="tpu_custom_call" | custom-call | tf_op jit(solution)/shard_map/store/pallas_call | solution.py:385
where the time goes:
time: 49.8 us; the launch traced here: 49.7 us
  Pallas kernels  49 us (98%)
  between operations  0.64 us (1%)
    pallas_call x1, Pallas kernels, local(): pl.pallas_call(functools.partial(kernel, tensors, workers), out_shape=[V(...  46.3 us
    pallas_call x1, Pallas kernels, local(): pl.pallas_call(store, out_shape=[S(shape, dtype) for shape, dtype in resu...  2.69 us

commit v1 on v0

v1 whole, which is shorter than its diff:
```python
import functools
import math

import jax
import jax.numpy as jnp
from jax import lax
from jax.experimental import pallas as pl
from jax.experimental.pallas import tpu as pltpu
from jax.sharding import PartitionSpec as P

DH = 128
CHUNKS = 8
DIRECT = 1
AHEAD = 5
SKEW = 3
SUM_LAG = 3
SPREAD_LAG = 3
UNROLL = 5
MID = 2
VMEM_BYTES = 67043328
SPARE = 2**17
MESH = pl.DeviceIdType.MESH

beta_first = 0.9
beta_second = 0.95
correct_first = 0.9999734386011124
correct_second = 0.994079470779666
inner_rate = 0.01
decay_rate = 0.1
epsilon = 1e-08
outer_rate = 0.7
outer_beta = 0.9

F32 = jnp.float32
BF16 = jnp.bfloat16


def dot(a, b, ca, cb):
    return lax.dot_general(a, b, (((ca,), (cb,)), ((), ())), preferred_element_type=F32)


def kernel(
    tensors,
    workers,
    q_hbm, k_hbm, v_hbm, g_hbm, w_hbm, m1_hbm, m2_hbm, anchor_hbm, mom_hbm,
    dq, dk, dv, n1, n2, na, nm,
    q, k, v, g, w, m1, m2, anchor, mom,
    probs, att, att_t, ds, delta, from_partner, pair, from_peers,
    in_sem,
    g_send, e_send, g_recv, p_send, p_recv, r_send, r_recv, a_send, a_recv, f_send, f_recv,
):
    heads = w.shape[0]
    width = g.shape[2]
    length = q.shape[0]
    slab = mom.shape[1]
    chips = workers // 2
    cw = width // CHUNKS
    scale = 1.0 / math.sqrt(DH)

    i = lax.axis_index("tensor")
    r = lax.axis_index("replica")
    chip = r // 2
    core = r % 2
    partner = chip * 2 + 1 - core
    has_left = i > 0
    has_right = i < tensors - 1

    def peer(step):
        return lax.rem(chip + step, chips) * 2 + core

    barrier = pltpu.get_barrier_semaphore()

    def other(step):
        return lax.rem(i + step, tensors)

    for step in range(1, tensors):
        pl.semaphore_signal(barrier, inc=1, device_id={"tensor": other(step)}, device_id_type=MESH)

    pl.semaphore_signal(barrier, inc=1, device_id={"replica": partner}, device_id_type=MESH)
    for step in range(1, chips):
        pl.semaphore_signal(barrier, inc=1, device_id={"replica": peer(step)}, device_id_type=MESH)

    loads = [
        pltpu.make_async_copy(s, d, in_sem.at[n])
        for n, (s, d) in enumerate(
            [
                (g_hbm, g.at[i]), (q_hbm, q), (k_hbm, k), (v_hbm, v), (w_hbm, w),
                (m1_hbm, m1), (m2_hbm, m2), (anchor_hbm, anchor), (mom_hbm, mom),
            ]
        )
    ]
    for load in loads:
        load.start()

    inner = jnp.logical_and(has_left, has_right)

    pl.semaphore_wait(barrier, tensors - 1 + chips)

    def cols(c):
        return pl.ds(pl.multiple_of(c * cw, cw), cw)

    def gather_copy(block, where, send, recv, target):
        piece = g.at[block, :, where]
        return pltpu.make_async_remote_copy(
            src_ref=piece, dst_ref=piece, send_sem=send, recv_sem=recv,
            device_id={"tensor": target}, device_id_type=MESH,
        )

    def right_copy(block, s, c):
        return gather_copy(block, cols(c), g_send.at[0, s], g_recv.at[block, c], i + 1)

    def left_copy(block, s, c):
        return gather_copy(block, cols(c), g_send.at[1, s], g_recv.at[block, c], i - 1)

    far_right = i < tensors - 2
    far_left = i > 1

    def own_first(c):
        if c < DIRECT:
            @pl.when(far_right)
            def _():
                gather_copy(i, cols(c), e_send.at[0], g_recv.at[i, c], tensors - 1).start()

            @pl.when(far_left)
            def _():
                gather_copy(i, cols(c), e_send.at[1], g_recv.at[i, c], 0).start()

        @pl.when(jnp.logical_and(has_right, jnp.logical_or(i == 0, c < AHEAD)))
        def _():
            right_copy(i, 0, c).start()

        @pl.when(jnp.logical_and(has_left, jnp.logical_or(i == tensors - 1, c < AHEAD)))
        def _():
            left_copy(i, 0, c).start()

    def own_later(n):
        c = n + AHEAD - SKEW * (i - 1)

        @pl.when(jnp.logical_and(inner, jnp.logical_and(c >= AHEAD, c < CHUNKS)))
        def _():
            right_copy(i, 0, c).start()

        e = n + AHEAD - SKEW * (tensors - 2 - i)

        @pl.when(jnp.logical_and(inner, jnp.logical_and(e >= AHEAD, e < CHUNKS)))
        def _():
            left_copy(i, 0, e).start()

    def relay(c, s):
        @pl.when(i - 1 - s >= 0)
        def _():
            block = i - 1 - s
            right_copy(block, s, c).wait_recv()
            if s + 1 <= tensors - 2:
                @pl.when(jnp.logical_or(far_right, c >= DIRECT))
                def _():
                    right_copy(block, s + 1, c).start()

        @pl.when(i + 1 + s < tensors)
        def _():
            block = i + 1 + s
            left_copy(block, s, c).wait_recv()
            if s + 1 <= tensors - 2:
                @pl.when(jnp.logical_or(far_left, c >= DIRECT))
                def _():
                    left_copy(block, s + 1, c).start()

    def arrive(c):
        for step in range(1, tensors):
            block = lax.rem(i + step, tensors)
            right_copy(block, 0, c).wait_recv()

    def drain_gather():
        start = pl.ds(0, DIRECT * cw)
        rest = pl.ds(DIRECT * cw, width - DIRECT * cw)
        every = pl.ds(0, width)
        if DIRECT > 0:
            @pl.when(far_right)
            def _():
                gather_copy(i, start, e_send.at[0], g_recv.at[i, 0], i).wait_send()

            @pl.when(far_left)
            def _():
                gather_copy(i, start, e_send.at[1], g_recv.at[i, 0], i).wait_send()

        for s in range(tensors - 1):
            for side, ok, far in ((0, has_right, far_right), (1, has_left, far_left)):
                block = i + s if side else i - s
                held = jnp.logical_and(block >= 0, block < tensors)
                ok = jnp.logical_and(ok, held)
                if s == 0:
                    far = ok

                @pl.when(jnp.logical_and(ok, far))
                def _():
                    gather_copy(block, every, g_send.at[side, s], g_recv.at[i, 0], i).wait_send()

                if s > 0:
                    @pl.when(jnp.logical_and(ok, jnp.logical_not(far)))
                    def _():
                        gather_copy(block, rest, g_send.at[side, s], g_recv.at[i, 0], i).wait_send()

    def head_cols(h):
        return pl.ds(pl.multiple_of(h * DH, DH), DH)

    def forward(h):
        hc = head_cols(h)
        s = dot(q[:, hc], k[:, hc], 1, 1) * scale
        e = jnp.exp(s - jnp.max(s, axis=-1, keepdims=True))
        p = (e / jnp.sum(e, axis=-1, keepdims=True)).astype(BF16)
        probs[h] = p
        a = dot(p, v[:, hc], 1, 0)
        att[:, hc] = a.astype(BF16)
        att_t[h] = a.T.astype(BF16)

    def adam(c):
        def body(h, carry):
            gb = g[:, :, cols(c)].reshape(length, cw)
            grad = dot(att_t[h], gb, 1, 0)
            first = beta_first * m1[h, :, cols(c)].astype(F32) + (1.0 - beta_first) * grad
            second = (
                beta_second * m2[h, :, cols(c)].astype(F32) + (1.0 - beta_second) * grad * grad
            )
            n1[h, :, cols(c)] = first.astype(BF16)
            n2[h, :, cols(c)] = second.astype(BF16)
            old = w[h, :, cols(c)].astype(F32)
            moved = (inner_rate / correct_first) * first / (
                jnp.sqrt(second * (1.0 / correct_second)) + epsilon
            )
            stepped = old * (1.0 - inner_rate * decay_rate) - moved
            an = anchor[h, :, :, cols(c)].astype(F32)
            d = an - stepped.reshape(workers, slab, cw)
            for x in range(workers):
                delta[c, x % 2, x // 2, h] = d[x].astype(BF16)
            return carry

        lax.fori_loop(0, heads, body, 0, unroll=UNROLL)

    def partner_copy(c):
        return pltpu.make_async_remote_copy(
            src_ref=delta.at[c, 1 - core], dst_ref=from_partner.at[c],
            send_sem=p_send, recv_sem=p_recv.at[c],
            device_id={"replica": partner}, device_id_type=MESH,
        )

    def peer_copy(c, step):
        return pltpu.make_async_remote_copy(
            src_ref=pair.at[c, lax.rem(chip + step, chips)], dst_ref=from_peers.at[c, step - 1],
            send_sem=r_send, recv_sem=r_recv.at[c],
            device_id={"replica": peer(step)}, device_id_type=MESH,
        )

    def pair_sum(c):
        partner_copy(c).wait_recv()
        for x in range(chips):
            pair[c, x] = (
                delta[c, core, x].astype(F32) + from_partner[c, x].astype(F32)
            ).astype(BF16)
        for step in range(1, chips):
            peer_copy(c, step).start()

    def spread(c, step):
        piece = na.at[:, chip, core, :, cols(c)]
        return pltpu.make_async_remote_copy(
            src_ref=piece, dst_ref=piece, send_sem=a_send, recv_sem=a_recv.at[c],
            device_id={"replica": peer(step)}, device_id_type=MESH,
        )

    def across(c, side):
        piece = na.at[:, :, side, :, cols(c)]
        return pltpu.make_async_remote_copy(
            src_ref=piece, dst_ref=piece, send_sem=f_send, recv_sem=f_recv.at[c],
            device_id={"replica": partner}, device_id_type=MESH,
        )

    def arrived(ref, sem):
        pltpu.make_async_copy(ref, ref, sem).wait()

    def outer(c):
        arrived(from_peers.at[c], r_recv.at[c])
        total = delta[c, core, chip].astype(F32) + from_partner[c, chip].astype(F32)
        for step in range(1, chips):
            total = total + from_peers[c, step - 1].astype(F32)
        average = total / workers
        moved = outer_beta * mom[:, :, cols(c)] + average
        nm[:, :, cols(c)] = moved
        part = anchor[:, r, :, cols(c)].astype(F32)
        na[:, chip, core, :, cols(c)] = (
            part - outer_rate * (average + outer_beta * moved)
        ).astype(BF16)
        for step in range(1, chips):
            spread(c, step).start()

    def pass_on(c):
        arrived(from_peers.at[c], a_recv.at[c])
        across(c, core).start()

    def finish(c):
        across(c, 1 - core).wait_recv()

    def backward(h):
        hc = head_cols(h)
        kh = k[:, hc]
        ga = dot(g[...].reshape(length, width), w[h], 1, 1).astype(BF16)
        row = jnp.sum(ga.astype(F32) * att[:, hc].astype(F32), axis=-1, keepdims=True)
        gp = dot(ga, v[:, hc], 1, 1)
        s = (probs[h].astype(F32) * (gp - row)).astype(BF16)
        ds[...] = s
        dq[:, hc] = (dot(s, kh, 1, 0) * scale).astype(BF16)
        dv[:, hc] = dot(ga, probs[h], 0, 0).T.astype(BF16)
        dk[:, hc] = (dot(q[:, hc], ds[...], 0, 0) * scale).T.astype(BF16)

    def within(n, count):
        return jnp.logical_and(n >= 0, n < count)

    loads[0].wait()
    for c in range(CHUNKS):
        own_first(c)
    for load in loads[1:4]:
        load.wait()
    for h in range(heads):
        forward(h)
    for load in loads[4:]:
        load.wait()

    far = jnp.maximum(i, tensors - 1 - i)
    lag = jnp.where(inner, SKEW * (far - 1) + MID, 0)
    early = jnp.where(inner, 0, DIRECT)
    summed = 1 + SUM_LAG
    spreads = summed + SPREAD_LAG

    def step(n, carry):
        for s in range(tensors - 1):
            c = n - SKEW * s

            @pl.when(jnp.logical_and(inner, within(c, CHUNKS)))
            def _():
                relay(c, s)

        own_later(n)

        m = n - lag

        if DIRECT > 0:
            @pl.when(jnp.logical_and(jnp.logical_not(inner), m == DIRECT))
            def _():
                pair_sum(DIRECT - 1)
                for c in range(DIRECT):
                    outer(c)
                for c in range(DIRECT):
                    pass_on(c)

        @pl.when(within(m, CHUNKS))
        def _():
            @pl.when(jnp.logical_not(inner))
            def _():
                arrive(m)

            adam(m)
            partner_copy(m).start()

        @pl.when(within(m - CHUNKS, heads))
        def _():
            backward(m - CHUNKS)

        @pl.when(jnp.logical_and(within(m - 1, CHUNKS), m != early))
        def _():
            pair_sum(m - 1)

        @pl.when(jnp.logical_and(m - summed >= early, m - summed < CHUNKS))
        def _():
            outer(m - summed)

        @pl.when(jnp.logical_and(m - spreads >= early, m - spreads < CHUNKS))
        def _():
            pass_on(m - spreads)

        return carry

    longest = SKEW * max(tensors - 3, 0) + MID
    lax.fori_loop(0, longest + CHUNKS + max(spreads, heads), step, 0)
    for c in range(CHUNKS):
        finish(c)
    drain_gather()
    arrived(from_partner, p_send)
    arrived(from_peers, r_send)
    arrived(from_peers, a_send)
    arrived(from_partner, f_send)


def store(*refs):
    n = (len(refs) - 1) // 2
    copies = [pltpu.make_async_copy(refs[j], refs[n + j], refs[-1].at[j]) for j in range(n)]
    for copy in copies:
        copy.start()
    for copy in copies:
        copy.wait()


def local(tensors, workers, queries, key_rows, value_rows, out_grads, inner_weights, adam_first,
          adam_second, anchor, momentum):
    length, inner = queries.shape[1:]
    rows, width = out_grads.shape[1:]
    heads = inner_weights.shape[1]
    slab = momentum.shape[1]
    chips = workers // 2
    cw = width // CHUNKS
    qs = (length, inner)
    ws = (heads, DH, width)
    an = (heads, workers, slab, width)
    ms = (heads, slab, width)
    S = jax.ShapeDtypeStruct
    hbm = pl.BlockSpec(memory_space=pltpu.HBM)
    V = pltpu.VMEM
    D = pltpu.SemaphoreType.DMA
    nas = (heads, chips, 2, slab, width)
    results = [(qs, BF16)] * 3 + [(ws, BF16)] * 2 + [(nas, BF16), (ms, F32)]
    held = sum(math.prod(shape) * jnp.dtype(dtype).itemsize for shape, dtype in results)
    room = VMEM_BYTES - held - SPARE
    outs = pl.pallas_call(
        functools.partial(kernel, tensors, workers),
        out_shape=[V(shape, dtype) for shape, dtype in results],
        in_specs=[hbm] * 9,
        out_specs=[pl.BlockSpec(memory_space=V)] * 7,
        scratch_shapes=[
            V(qs, BF16), V(qs, BF16), V(qs, BF16), V((tensors, rows, width), BF16),
            V(ws, BF16), V(ws, BF16), V(ws, BF16), V(an, BF16), V(ms, F32),
            V((heads, length, length), BF16), V(qs, BF16), V((heads, DH, length), BF16),
            V((length, length), BF16),
            V((CHUNKS, 2, chips, heads, slab, cw), BF16),
            V((CHUNKS, chips, heads, slab, cw), BF16),
            V((CHUNKS, chips, heads, slab, cw), BF16),
            V((CHUNKS, chips - 1, heads, slab, cw), BF16),
            D((9,)),
            D((2, tensors - 1)), D((2,)), D((tensors, CHUNKS)),
            D, D((CHUNKS,)), D, D((CHUNKS,)), D, D((CHUNKS,)), D, D((CHUNKS,)),
        ],
        compiler_params=pltpu.CompilerParams(collective_id=0, has_side_effects=True, vmem_limit_bytes=room),
        name="sync",
    )(
        queries[0], key_rows[0], value_rows[0], out_grads[0], inner_weights[0], adam_first[0],
        adam_second[0], anchor.reshape(an), momentum,
    )
    dq, dk, dv, n1, n2, na, nm = pl.pallas_call(
        store,
        out_shape=[S(shape, dtype) for shape, dtype in results],
        in_specs=[pl.BlockSpec(memory_space=V)] * 7,
        out_specs=[hbm] * 7,
        scratch_shapes=[D((7,))],
        compiler_params=pltpu.CompilerParams(vmem_limit_bytes=2**20),
        name="store",
    )(*outs)
    return dq[None], dk[None], dv[None], n1[None], n2[None], na.reshape(anchor.shape), nm


def solution(mesh):
    workers = P("replica", "tensor", None, None)
    heads = P("replica", None, "tensor")
    specs = (
        heads, heads, heads, P("replica", "tensor", None), workers, workers, workers,
        P("tensor", None, None), P("tensor", "replica", None),
    )
    outs = (
        heads, heads, heads, workers, workers, P("tensor", None, None), P("tensor", "replica", None)
    )
    body = functools.partial(local, mesh.shape["tensor"], mesh.shape["replica"])
    return jax.shard_map(body, mesh=mesh, in_specs=specs, out_specs=outs, check_vma=False)
```

time: 49.8 us -> 41.7 us (0.84)
  Pallas kernels: 49 us -> 40.9 us
    pallas_call x1, Pallas kernels: 46.3 us -> 38.2 us  [local(): pl.pallas_call(functools.partial(kernel, tensors, workers), out_shape=[V(...]
where the time goes in v1:
time: 41.7 us; the launch traced here: 41.6 us
  Pallas kernels  40.9 us (98%)
  between operations  0.64 us (2%)
    pallas_call x1, Pallas kernels, local(): pl.pallas_call(functools.partial(kernel, tensors, workers), out_shape=[V(...  38.2 us
    pallas_call x1, Pallas kernels, local(): pl.pallas_call(store, out_shape=[S(shape, dtype) for shape, dtype in resu...  2.69 us

profile of v1, /device:TPU:0, one launch (start us, length us, event | category | flops | bytes accessed | tf_op | source)
XLA Modules:
  0.0 41.6 jit_solution(9720474410560312441)
XLA Ops:
  0.6 38.2 %sync.1 = (bf16[512,640]{1,0:T(8,128)(2,1)S(1)}, bf16[512,640]{1,0:T(8,128)(2,1)S(1)}, bf16[512,640]{1,0:T(8,128)(2,1)S(1)}, bf16[5,128,1024]{2,1,0:T(8,128)(2,1...) custom-call(bf16[512,640]{1,0:T(8,128)(2,1)} %bitcast.18, ...), custom_call_target="tpu_custom_call" | custom-call | tf_op jit(solution)/shard_map/sync/pallas_call | solution.py:420
  38.9 2.7 %store.1 = (bf16[512,640]{1,0:T(8,128)(2,1)}, bf16[512,640]{1,0:T(8,128)(2,1)}, bf16[512,640]{1,0:T(8,128)(2,1)}, bf16[5,128,1024]{2,1,0:T(8,128)(2,1)}, bf16[5,...) custom-call(bf16[512,640]{1,0:T(8,128)(2,1)S(1)} %get-tuple-element.21.refs_0_, ...), custom_call_target="tpu_custom_call" | custom-call | tf_op jit(solution)/shard_map/store/pallas_call | solution.py:444

commit v2 on v1

--- a/solution.py
+++ b/solution.py
@@ -10,13 +10,21 @@
 
 DH = 128
 CHUNKS = 8
-DIRECT = 1
-AHEAD = 5
-SKEW = 3
+DIRECT = 2
+AHEAD = 3
+AHEAD_END = 6
+AHEAD1 = 4
+AHEAD_END1 = 5
+SKEW = 2
 SUM_LAG = 3
-SPREAD_LAG = 3
+SPREAD_LAG = 6
 UNROLL = 5
-MID = 2
+MID = 0
+RIGHT = 0
+TURN = 2
+EARLY = 2
+NEAR_AT = 1
+FAR_AT = 3
 VMEM_BYTES = 67043328
 SPARE = 2**17
 MESH = pl.DeviceIdType.MESH
@@ -45,9 +53,9 @@
     q_hbm, k_hbm, v_hbm, g_hbm, w_hbm, m1_hbm, m2_hbm, anchor_hbm, mom_hbm,
     dq, dk, dv, n1, n2, na, nm,
     q, k, v, g, w, m1, m2, anchor, mom,
-    probs, att, att_t, ds, delta, from_partner, pair, from_peers,
+    probs, att, att_t, ds, gs, gacc, delta, from_partner, pair, from_peers,
     in_sem,
-    g_send, e_send, g_recv, p_send, p_recv, r_send, r_recv, a_send, a_recv, f_send, f_recv,
+    near, far_end, side, g_send, e_send, g_recv, p_send, p_recv, r_send, r_recv, a_send, a_recv, f_send, f_recv,
 ):
     heads = w.shape[0]
     width = g.shape[2]
@@ -70,15 +78,19 @@
 
     barrier = pltpu.get_barrier_semaphore()
 
-    def other(step):
-        return lax.rem(i + step, tensors)
-
     for step in range(1, tensors):
-        pl.semaphore_signal(barrier, inc=1, device_id={"tensor": other(step)}, device_id_type=MESH)
-
-    pl.semaphore_signal(barrier, inc=1, device_id={"replica": partner}, device_id_type=MESH)
+        @pl.when(i + step < tensors)
+        def _():
+            pl.semaphore_signal(barrier, inc=1, device_id={"tensor": i + step}, device_id_type=MESH)
+
+    @pl.when(core == 0)
+    def _():
+        pl.semaphore_signal(barrier, inc=1, device_id={"replica": partner}, device_id_type=MESH)
+
     for step in range(1, chips):
-        pl.semaphore_signal(barrier, inc=1, device_id={"replica": peer(step)}, device_id_type=MESH)
+        @pl.when(chip + step < chips)
+        def _():
+            pl.semaphore_signal(barrier, inc=1, device_id={"replica": peer(step)}, device_id_type=MESH)
 
     loads = [
         pltpu.make_async_copy(s, d, in_sem.at[n])
@@ -94,7 +106,27 @@
 
     inner = jnp.logical_and(has_left, has_right)
 
-    pl.semaphore_wait(barrier, tensors - 1 + chips)
+    @pl.when(i + chip + core > 0)
+    def _():
+        pl.semaphore_wait(barrier, i + chip + core)
+
+    @pl.when(has_left)
+    def _():
+        pl.semaphore_signal(near, inc=1, device_id={"tensor": i - 1}, device_id_type=MESH)
+
+    @pl.when(core == 1)
+    def _():
+        pl.semaphore_signal(side, inc=1, device_id={"replica": partner}, device_id_type=MESH)
+
+    for step in range(1, chips):
+        @pl.when(chip + step >= chips)
+        def _():
+            pl.semaphore_signal(side, inc=1, device_id={"replica": peer(step)}, device_id_type=MESH)
+
+    for step in range(2, tensors):
+        @pl.when(jnp.logical_and(i == tensors - 1, i - step >= 0))
+        def _():
+            pl.semaphore_signal(far_end, inc=1, device_id={"tensor": i - step}, device_id_type=MESH)
 
     def cols(c):
         return pl.ds(pl.multiple_of(c * cw, cw), cw)
@@ -115,55 +147,85 @@
     far_right = i < tensors - 2
     far_left = i > 1
 
-    def own_first(c):
-        if c < DIRECT:
+    def turned(c):
+        return lax.rem(c + TURN, CHUNKS)
+
+    def own_right(n):
+        right_copy(i, 0, jnp.where(far_right, turned(n), n)).start()
+
+    def own_left(n):
+        left_copy(i, 0, jnp.where(far_left, turned(n), n)).start()
+
+    ahead = jnp.where(core == 0, AHEAD, AHEAD1)
+    ahead_end = jnp.where(core == 0, AHEAD_END, AHEAD_END1)
+    ahead_right = jnp.where(i == 0, CHUNKS, jnp.where(far_right, ahead, ahead_end))
+    ahead_left = jnp.where(i == tensors - 1, CHUNKS, jnp.where(far_left, ahead, ahead_end))
+
+    def first_left():
+        for n in range(CHUNKS):
+            @pl.when(jnp.logical_and(i == 1, n < ahead_left))
+            def _():
+                own_left(n)
+
+            if n < DIRECT:
+                @pl.when(far_left)
+                def _():
+                    gather_copy(i, cols(n), e_send.at[1], g_recv.at[i, n], 0).start()
+
+        for n in range(CHUNKS):
+            @pl.when(jnp.logical_and(far_left, n < ahead_left))
+            def _():
+                own_left(n)
+
+    def first_near():
+        @pl.when(has_right)
+        def _():
+            pl.semaphore_wait(near, 1)
+
+        for n in range(CHUNKS):
+            @pl.when(jnp.logical_and(has_right, n < ahead_right))
+            def _():
+                own_right(n)
+
+    def first_far():
+        @pl.when(far_right)
+        def _():
+            pl.semaphore_wait(far_end, 1)
+
+        for n in range(DIRECT):
             @pl.when(far_right)
             def _():
-                gather_copy(i, cols(c), e_send.at[0], g_recv.at[i, c], tensors - 1).start()
-
-            @pl.when(far_left)
-            def _():
-                gather_copy(i, cols(c), e_send.at[1], g_recv.at[i, c], 0).start()
-
-        @pl.when(jnp.logical_and(has_right, jnp.logical_or(i == 0, c < AHEAD)))
-        def _():
-            right_copy(i, 0, c).start()
-
-        @pl.when(jnp.logical_and(has_left, jnp.logical_or(i == tensors - 1, c < AHEAD)))
-        def _():
-            left_copy(i, 0, c).start()
-
-    def own_later(n):
-        c = n + AHEAD - SKEW * (i - 1)
-
-        @pl.when(jnp.logical_and(inner, jnp.logical_and(c >= AHEAD, c < CHUNKS)))
-        def _():
-            right_copy(i, 0, c).start()
-
-        e = n + AHEAD - SKEW * (tensors - 2 - i)
-
-        @pl.when(jnp.logical_and(inner, jnp.logical_and(e >= AHEAD, e < CHUNKS)))
-        def _():
-            left_copy(i, 0, e).start()
-
-    def relay(c, s):
-        @pl.when(i - 1 - s >= 0)
-        def _():
-            block = i - 1 - s
-            right_copy(block, s, c).wait_recv()
-            if s + 1 <= tensors - 2:
-                @pl.when(jnp.logical_or(far_right, c >= DIRECT))
-                def _():
-                    right_copy(block, s + 1, c).start()
-
-        @pl.when(i + 1 + s < tensors)
-        def _():
-            block = i + 1 + s
-            left_copy(block, s, c).wait_recv()
-            if s + 1 <= tensors - 2:
-                @pl.when(jnp.logical_or(far_left, c >= DIRECT))
-                def _():
-                    left_copy(block, s + 1, c).start()
+                gather_copy(i, cols(n), e_send.at[0], g_recv.at[i, n], tensors - 1).start()
+
+    def later_right(n):
+        c = n + ahead_right - SKEW * (i - 1)
+
+        @pl.when(jnp.logical_and(inner, jnp.logical_and(c >= ahead_right, c < CHUNKS)))
+        def _():
+            own_right(c)
+
+    def later_left(n):
+        c = n + ahead_left - SKEW * (tensors - 2 - i)
+
+        @pl.when(jnp.logical_and(inner, jnp.logical_and(c >= ahead_left, c < CHUNKS)))
+        def _():
+            own_left(c)
+
+    def relay_right(c, s):
+        block = i - 1 - s
+        right_copy(block, s, c).wait_recv()
+        if s + 1 <= tensors - 2:
+            @pl.when(jnp.logical_or(far_right, c >= DIRECT))
+            def _():
+                right_copy(block, s + 1, c).start()
+
+    def relay_left(c, s):
+        block = i + 1 + s
+        left_copy(block, s, c).wait_recv()
+        if s + 1 <= tensors - 2:
+            @pl.when(jnp.logical_or(far_left, c >= DIRECT))
+            def _():
+                left_copy(block, s + 1, c).start()
 
     def arrive(c):
         for step in range(1, tensors):
@@ -224,9 +286,8 @@
             n1[h, :, cols(c)] = first.astype(BF16)
             n2[h, :, cols(c)] = second.astype(BF16)
             old = w[h, :, cols(c)].astype(F32)
-            moved = (inner_rate / correct_first) * first / (
-                jnp.sqrt(second * (1.0 / correct_second)) + epsilon
-            )
+            power = second * (1.0 / correct_second)
+            moved = (inner_rate / correct_first) * first / (power * lax.rsqrt(power) + epsilon)
             stepped = old * (1.0 - inner_rate * decay_rate) - moved
             an = anchor[h, :, :, cols(c)].astype(F32)
             d = an - stepped.reshape(workers, slab, cw)
@@ -298,10 +359,16 @@
     def finish(c):
         across(c, 1 - core).wait_recv()
 
+    def weigh(c):
+        part = pl.ds(pl.multiple_of(c * cw, cw), 2 * cw)
+        return dot(
+            g[:, :, part].reshape(length, 2 * cw), w[:, :, part].reshape(heads * DH, 2 * cw), 1, 1
+        )
+
     def backward(h):
         hc = head_cols(h)
         kh = k[:, hc]
-        ga = dot(g[...].reshape(length, width), w[h], 1, 1).astype(BF16)
+        ga = gs[:, hc]
         row = jnp.sum(ga.astype(F32) * att[:, hc].astype(F32), axis=-1, keepdims=True)
         gp = dot(ga, v[:, hc], 1, 1)
         s = (probs[h].astype(F32) * (gp - row)).astype(BF16)
@@ -314,41 +381,58 @@
         return jnp.logical_and(n >= 0, n < count)
 
     loads[0].wait()
-    for c in range(CHUNKS):
-        own_first(c)
+    first_left()
     for load in loads[1:4]:
         load.wait()
     for h in range(heads):
+        if h == min(NEAR_AT, heads - 1):
+            first_near()
+        if h == min(FAR_AT, heads - 1):
+            first_far()
         forward(h)
     for load in loads[4:]:
         load.wait()
 
-    far = jnp.maximum(i, tensors - 1 - i)
-    lag = jnp.where(inner, SKEW * (far - 1) + MID, 0)
-    early = jnp.where(inner, 0, DIRECT)
+    @pl.when(chips - chip - core > 0)
+    def _():
+        pl.semaphore_wait(side, chips - chip - core)
+
+
+    behind = jnp.maximum(SKEW * (i - 1) + RIGHT, SKEW * (tensors - 2 - i))
+    lag = jnp.where(inner, behind + MID, 0)
+    early = jnp.where(inner, 0, EARLY)
     summed = 1 + SUM_LAG
     spreads = summed + SPREAD_LAG
+
+    def order(c):
+        return jnp.where(inner, turned(c), c)
 
     def step(n, carry):
         for s in range(tensors - 1):
             c = n - SKEW * s
 
-            @pl.when(jnp.logical_and(inner, within(c, CHUNKS)))
-            def _():
-                relay(c, s)
-
-        own_later(n)
+            @pl.when(jnp.logical_and(inner, jnp.logical_and(i + 1 + s < tensors, within(c, CHUNKS))))
+            def _():
+                relay_left(turned(c), s)
+
+        later_left(n)
+        for s in range(tensors - 1):
+            c = n - RIGHT - SKEW * s
+
+            @pl.when(jnp.logical_and(inner, jnp.logical_and(i - 1 - s >= 0, within(c, CHUNKS))))
+            def _():
+                relay_right(turned(c), s)
+
+        later_right(n - RIGHT)
 
         m = n - lag
 
-        if DIRECT > 0:
-            @pl.when(jnp.logical_and(jnp.logical_not(inner), m == DIRECT))
-            def _():
+        @pl.when(jnp.logical_and(jnp.logical_not(inner), m == DIRECT))
+        def _():
+            if DIRECT > 0:
                 pair_sum(DIRECT - 1)
-                for c in range(DIRECT):
-                    outer(c)
-                for c in range(DIRECT):
-                    pass_on(c)
+            for c in range(EARLY):
+                outer(c)
 
         @pl.when(within(m, CHUNKS))
         def _():
@@ -356,29 +440,41 @@
             def _():
                 arrive(m)
 
-            adam(m)
-            partner_copy(m).start()
-
-        @pl.when(within(m - CHUNKS, heads))
-        def _():
-            backward(m - CHUNKS)
-
-        @pl.when(jnp.logical_and(within(m - 1, CHUNKS), m != early))
-        def _():
-            pair_sum(m - 1)
+            adam(order(m))
+            partner_copy(order(m)).start()
+
+        @pl.when(m == 2)
+        def _():
+            gacc[...] = weigh(order(0))
+
+        @pl.when(jnp.logical_and(lax.rem(m + CHUNKS, 2) == 0, jnp.logical_and(m > 2, m < CHUNKS - 2)))
+        def _():
+            gacc[...] += weigh(order(m - 2))
+
+        @pl.when(m == CHUNKS)
+        def _():
+            gs[...] = (gacc[...] + weigh(order(CHUNKS - 4)) + weigh(order(CHUNKS - 2))).astype(BF16)
+
+        @pl.when(within(m - CHUNKS - 1, heads))
+        def _():
+            backward(m - CHUNKS - 1)
+
+        @pl.when(jnp.logical_and(within(m - 1, CHUNKS), jnp.logical_or(inner, m != DIRECT)))
+        def _():
+            pair_sum(order(m - 1))
 
         @pl.when(jnp.logical_and(m - summed >= early, m - summed < CHUNKS))
         def _():
-            outer(m - summed)
-
-        @pl.when(jnp.logical_and(m - spreads >= early, m - spreads < CHUNKS))
-        def _():
-            pass_on(m - spreads)
+            outer(order(m - summed))
+
+        @pl.when(within(m - spreads, CHUNKS))
+        def _():
+            pass_on(order(m - spreads))
 
         return carry
 
-    longest = SKEW * max(tensors - 3, 0) + MID
-    lax.fori_loop(0, longest + CHUNKS + max(spreads, heads), step, 0)
+    longest = SKEW * max(tensors - 3, 0) + RIGHT + MID
+    lax.fori_loop(0, longest + CHUNKS + max(spreads, heads + 1), step, 0)
     for c in range(CHUNKS):
         finish(c)
     drain_gather()
@@ -426,12 +522,13 @@
             V(qs, BF16), V(qs, BF16), V(qs, BF16), V((tensors, rows, width), BF16),
             V(ws, BF16), V(ws, BF16), V(ws, BF16), V(an, BF16), V(ms, F32),
             V((heads, length, length), BF16), V(qs, BF16), V((heads, DH, length), BF16),
-            V((length, length), BF16),
+            V((length, length), BF16), V((length, heads * DH), BF16), V((length, heads * DH), F32),
             V((CHUNKS, 2, chips, heads, slab, cw), BF16),
             V((CHUNKS, chips, heads, slab, cw), BF16),
             V((CHUNKS, chips, heads, slab, cw), BF16),
             V((CHUNKS, chips - 1, heads, slab, cw), BF16),
             D((9,)),
+            pltpu.SemaphoreType.REGULAR, pltpu.SemaphoreType.REGULAR, pltpu.SemaphoreType.REGULAR,
             D((2, tensors - 1)), D((2,)), D((tensors, CHUNKS)),
             D, D((CHUNKS,)), D, D((CHUNKS,)), D, D((CHUNKS,)), D, D((CHUNKS,)),
         ],

time: 41.7 us -> 38.7 us (0.928)
  Pallas kernels: 40.9 us -> 37.9 us
    pallas_call x1, Pallas kernels: 38.2 us -> 35.2 us  [local(): pl.pallas_call(functools.partial(kernel, tensors, workers), out_shape=[V(...]
where the time goes in v2:
time: 38.7 us; the launch traced here: 38.5 us
  Pallas kernels  37.9 us (98%)
  between operations  0.64 us (2%)
    pallas_call x1, Pallas kernels, local(): pl.pallas_call(functools.partial(kernel, tensors, workers), out_shape=[V(...  35.2 us
    pallas_call x1, Pallas kernels, local(): pl.pallas_call(store, out_shape=[S(shape, dtype) for shape, dtype in resu...  2.69 us

profile of v2, /device:TPU:0, one launch (start us, length us, event | category | flops | bytes accessed | tf_op | source)
XLA Modules:
  0.0 38.5 jit_solution(15192836881124498046)
XLA Ops:
  0.6 35.2 %sync.1 = (bf16[512,640]{1,0:T(8,128)(2,1)S(1)}, bf16[512,640]{1,0:T(8,128)(2,1)S(1)}, bf16[512,640]{1,0:T(8,128)(2,1)S(1)}, bf16[5,128,1024]{2,1,0:T(8,128)(2,1...) custom-call(bf16[512,640]{1,0:T(8,128)(2,1)} %bitcast.18, ...), custom_call_target="tpu_custom_call" | custom-call | tf_op jit(solution)/shard_map/sync/pallas_call | solution.py:516
  35.8 2.7 %store.1 = (bf16[512,640]{1,0:T(8,128)(2,1)}, bf16[512,640]{1,0:T(8,128)(2,1)}, bf16[512,640]{1,0:T(8,128)(2,1)}, bf16[5,128,1024]{2,1,0:T(8,128)(2,1)}, bf16[5,...) custom-call(bf16[512,640]{1,0:T(8,128)(2,1)S(1)} %get-tuple-element.21.refs_0_, ...), custom_call_target="tpu_custom_call" | custom-call | tf_op jit(solution)/shard_map/store/pallas_call | solution.py:541

commit v3 on v2

--- a/solution.py
+++ b/solution.py
@@ -12,7 +12,7 @@
 CHUNKS = 8
 DIRECT = 2
 AHEAD = 3
-AHEAD_END = 6
+AHEAD_END = 7
 AHEAD1 = 4
 AHEAD_END1 = 5
 SKEW = 2
@@ -22,6 +22,8 @@
 MID = 0
 RIGHT = 0
 TURN = 2
+SKEW_RIGHT = 2
+RIGHT_FIRST = True
 EARLY = 2
 NEAR_AT = 1
 FAR_AT = 3
@@ -142,7 +144,7 @@
         return gather_copy(block, cols(c), g_send.at[0, s], g_recv.at[block, c], i + 1)
 
     def left_copy(block, s, c):
-        return gather_copy(block, cols(c), g_send.at[1, s], g_recv.at[block, c], i - 1)
+        return gather_copy(block, cols(c), g_send.at[1, s], g_recv.at[block - 1, c], i - 1)
 
     far_right = i < tensors - 2
     far_left = i > 1
@@ -170,7 +172,7 @@
             if n < DIRECT:
                 @pl.when(far_left)
                 def _():
-                    gather_copy(i, cols(n), e_send.at[1], g_recv.at[i, n], 0).start()
+                    gather_copy(i, cols(n), e_send.at[1], g_recv.at[i - 1, n], 0).start()
 
         for n in range(CHUNKS):
             @pl.when(jnp.logical_and(far_left, n < ahead_left))
@@ -198,7 +200,7 @@
                 gather_copy(i, cols(n), e_send.at[0], g_recv.at[i, n], tensors - 1).start()
 
     def later_right(n):
-        c = n + ahead_right - SKEW * (i - 1)
+        c = n + ahead_right - SKEW_RIGHT * (i - 1)
 
         @pl.when(jnp.logical_and(inner, jnp.logical_and(c >= ahead_right, c < CHUNKS)))
         def _():
@@ -230,7 +232,7 @@
     def arrive(c):
         for step in range(1, tensors):
             block = lax.rem(i + step, tensors)
-            right_copy(block, 0, c).wait_recv()
+            arrived(g.at[block, :, cols(c)], g_recv.at[block - jnp.where(block > i, 1, 0), c])
 
     def drain_gather():
         start = pl.ds(0, DIRECT * cw)
@@ -239,11 +241,11 @@
         if DIRECT > 0:
             @pl.when(far_right)
             def _():
-                gather_copy(i, start, e_send.at[0], g_recv.at[i, 0], i).wait_send()
+                gather_copy(i, start, e_send.at[0], g_recv.at[0, 0], i).wait_send()
 
             @pl.when(far_left)
             def _():
-                gather_copy(i, start, e_send.at[1], g_recv.at[i, 0], i).wait_send()
+                gather_copy(i, start, e_send.at[1], g_recv.at[0, 0], i).wait_send()
 
         for s in range(tensors - 1):
             for side, ok, far in ((0, has_right, far_right), (1, has_left, far_left)):
@@ -255,12 +257,12 @@
 
                 @pl.when(jnp.logical_and(ok, far))
                 def _():
-                    gather_copy(block, every, g_send.at[side, s], g_recv.at[i, 0], i).wait_send()
+                    gather_copy(block, every, g_send.at[side, s], g_recv.at[0, 0], i).wait_send()
 
                 if s > 0:
                     @pl.when(jnp.logical_and(ok, jnp.logical_not(far)))
                     def _():
-                        gather_copy(block, rest, g_send.at[side, s], g_recv.at[i, 0], i).wait_send()
+                        gather_copy(block, rest, g_send.at[side, s], g_recv.at[0, 0], i).wait_send()
 
     def head_cols(h):
         return pl.ds(pl.multiple_of(h * DH, DH), DH)
@@ -330,7 +332,7 @@
     def across(c, side):
         piece = na.at[:, :, side, :, cols(c)]
         return pltpu.make_async_remote_copy(
-            src_ref=piece, dst_ref=piece, send_sem=f_send, recv_sem=f_recv.at[c],
+            src_ref=piece, dst_ref=piece, send_sem=f_send, recv_sem=f_recv,
             device_id={"replica": partner}, device_id_type=MESH,
         )
 
@@ -356,9 +358,6 @@
         arrived(from_peers.at[c], a_recv.at[c])
         across(c, core).start()
 
-    def finish(c):
-        across(c, 1 - core).wait_recv()
-
     def weigh(c):
         part = pl.ds(pl.multiple_of(c * cw, cw), 2 * cw)
         return dot(
@@ -398,7 +397,7 @@
         pl.semaphore_wait(side, chips - chip - core)
 
 
-    behind = jnp.maximum(SKEW * (i - 1) + RIGHT, SKEW * (tensors - 2 - i))
+    behind = jnp.maximum(SKEW_RIGHT * (i - 1) + RIGHT, SKEW * (tensors - 2 - i))
     lag = jnp.where(inner, behind + MID, 0)
     early = jnp.where(inner, 0, EARLY)
     summed = 1 + SUM_LAG
@@ -408,21 +407,28 @@
         return jnp.where(inner, turned(c), c)
 
     def step(n, carry):
+        def go_left(s):
+            c = n - SKEW * s
+
+            @pl.when(jnp.logical_and(inner, jnp.logical_and(i + 1 + s < tensors, within(c, CHUNKS))))
+            def _():
+                relay_left(turned(c), s)
+
+        def go_right(s):
+            c = n - RIGHT - SKEW_RIGHT * s
+
+            @pl.when(jnp.logical_and(inner, jnp.logical_and(i - 1 - s >= 0, within(c, CHUNKS))))
+            def _():
+                relay_right(turned(c), s)
+
         for s in range(tensors - 1):
-            c = n - SKEW * s
-
-            @pl.when(jnp.logical_and(inner, jnp.logical_and(i + 1 + s < tensors, within(c, CHUNKS))))
-            def _():
-                relay_left(turned(c), s)
-
+            if s == 0 and RIGHT_FIRST:
+                go_right(s)
+                go_left(s)
+            else:
+                go_left(s)
+                go_right(s)
         later_left(n)
-        for s in range(tensors - 1):
-            c = n - RIGHT - SKEW * s
-
-            @pl.when(jnp.logical_and(inner, jnp.logical_and(i - 1 - s >= 0, within(c, CHUNKS))))
-            def _():
-                relay_right(turned(c), s)
-
         later_right(n - RIGHT)
 
         m = n - lag
@@ -473,10 +479,9 @@
 
         return carry
 
-    longest = SKEW * max(tensors - 3, 0) + RIGHT + MID
+    longest = max(SKEW, SKEW_RIGHT) * max(tensors - 3, 0) + RIGHT + MID
     lax.fori_loop(0, longest + CHUNKS + max(spreads, heads + 1), step, 0)
-    for c in range(CHUNKS):
-        finish(c)
+    arrived(from_partner, f_recv)
     drain_gather()
     arrived(from_partner, p_send)
     arrived(from_peers, r_send)
@@ -529,8 +534,8 @@
             V((CHUNKS, chips - 1, heads, slab, cw), BF16),
             D((9,)),
             pltpu.SemaphoreType.REGULAR, pltpu.SemaphoreType.REGULAR, pltpu.SemaphoreType.REGULAR,
-            D((2, tensors - 1)), D((2,)), D((tensors, CHUNKS)),
-            D, D((CHUNKS,)), D, D((CHUNKS,)), D, D((CHUNKS,)), D, D((CHUNKS,)),
+            D((2, tensors - 1)), D((2,)), D((tensors - 1, CHUNKS)),
+            D, D((CHUNKS,)), D, D((CHUNKS,)), D, D((CHUNKS,)), D, D,
         ],
         compiler_params=pltpu.CompilerParams(collective_id=0, has_side_effects=True, vmem_limit_bytes=room),
         name="sync",

time: 38.7 us -> 38.4 us (level)
  no operation moved by 1% of the time
where the time goes in v3:
time: 38.4 us; the launch traced here: 38.2 us
  Pallas kernels  37.6 us (98%)
  between operations  0.64 us (2%)
    pallas_call x1, Pallas kernels, local(): pl.pallas_call(functools.partial(kernel, tensors, workers), out_shape=[V(...  34.9 us
    pallas_call x1, Pallas kernels, local(): pl.pallas_call(store, out_shape=[S(shape, dtype) for shape, dtype in resu...  2.69 us

profile of v3, /device:TPU:0, one launch (start us, length us, event | category | flops | bytes accessed | tf_op | source)
XLA Modules:
  0.0 38.2 jit_solution(10118744676164753489)
XLA Ops:
  0.6 34.9 %sync.1 = (bf16[512,640]{1,0:T(8,128)(2,1)S(1)}, bf16[512,640]{1,0:T(8,128)(2,1)S(1)}, bf16[512,640]{1,0:T(8,128)(2,1)S(1)}, bf16[5,128,1024]{2,1,0:T(8,128)(2,1...) custom-call(bf16[512,640]{1,0:T(8,128)(2,1)} %bitcast.18, ...), custom_call_target="tpu_custom_call" | custom-call | tf_op jit(solution)/shard_map/sync/pallas_call | solution.py:521
  35.5 2.7 %store.1 = (bf16[512,640]{1,0:T(8,128)(2,1)}, bf16[512,640]{1,0:T(8,128)(2,1)}, bf16[512,640]{1,0:T(8,128)(2,1)}, bf16[5,128,1024]{2,1,0:T(8,128)(2,1)}, bf16[5,...) custom-call(bf16[512,640]{1,0:T(8,128)(2,1)S(1)} %get-tuple-element.21.refs_0_, ...), custom_call_target="tpu_custom_call" | custom-call | tf_op jit(solution)/shard_map/store/pallas_call | solution.py:546
